TPU v7x, 32 devices: a whole 2x2x4 slice. The times are simulated.
32 devices in a mesh: groups: 2 (over y), obs: 4 (over z), hid: 2 (over x), rep: 2 (over core).
Axes of the slice: x: 2, y: 2, z: 4, core: 2. Of those that a mesh axis runs over, the one named last changes fastest.
Arguments:
- particles: float32 [8, 128, 512], P(('groups', 'obs')), parts along dimension 0, may hold values from -6 to 6
- obs_embed: bfloat16 [32768, 256], P(('groups', 'obs', 'rep')), parts along dimension 0, may hold values from -6 to 6
- step_index: int32 [2], P('groups'), parts along dimension 0, may hold values from 1 to 63
- noise: float32 [8, 128, 512], P('groups', 'obs'), parts along dimension 0, may hold values from -6 to 6
- w_query: bfloat16 [512, 2048], P(None, 'hid'), may hold values from -0.25 to 0.25
- w_key: bfloat16 [256, 2048], P(None, 'hid'), may hold values from -0.375 to 0.375
- w_value: bfloat16 [256, 2048], P(None, 'hid'), may hold values from -0.375 to 0.375
- w_time: bfloat16 [256, 16], P(None, 'hid'), may hold values from -0.375 to 0.375
- w_score: bfloat16 [2048, 512], P('hid'), may hold values from -0.0009765625 to 0.0009765625
- prior_in: bfloat16 [512, 2048], P(None, 'hid'), may hold values from -0.25 to 0.25
- prior_time: bfloat16 [256, 2048], P(None, 'hid'), may hold values from -0.375 to 0.375
- prior_out: bfloat16 [2048, 512], P('hid'), may hold values from -7.6293945e-06 to 7.6293945e-06
Outputs:
- updated: float32 [8, 128, 512], P('groups', 'obs'), parts along dimension 0
- score_total: float32 [8, 128, 512], P('groups', 'obs'), parts along dimension 0
There are 2 independent parts, one for each index of `groups`. A program takes and returns all parts, laid end to end along the dimension named above; an argument that names none is the same for every part. Nothing has to cross between parts.
All inputs are finite; a program needn't handle non-finite values.
Results may differ from a plain program's by a relative error of at most 0.0042.
Values may be sent and summed in bfloat16 or wider, within the bound.
No kernel may reach another device: no remote copies, remote signals or barrier semaphores. Data moves between devices by JAX's collectives and lax.ppermute only.
A program may use at most 64 MiB of HBM per device.

v0:
```python
import math
import jax
import jax.numpy as jnp
from jax import lax
from jax.sharding import PartitionSpec as P

DH = 128
STEPS = 64
SIG_LO = 0.05
SIG_HI = 1.0


def passed_along(shard, axis, by):
    size = lax.axis_size(axis)
    return lax.ppermute(shard, axis, [(i, (i + by) % size) for i in range(size)])


def plan(step_index, feature_count):
    level = step_index[0].astype(jnp.float32)
    growth = math.log(SIG_HI / SIG_LO) / (STEPS - 1)
    sigma_now = SIG_LO * jnp.exp(growth * level)
    sigma_prev = SIG_LO * jnp.exp(growth * (level - 1.0))
    delta = sigma_now * sigma_now - sigma_prev * sigma_prev
    halves = feature_count // 2
    frequency = jnp.exp(-math.log(1000.0) / halves * jnp.arange(halves).astype(jnp.float32))
    angles = 10.0 * jnp.log(sigma_now) * frequency
    features = jnp.concatenate([jnp.sin(angles), jnp.cos(angles)])[None, :].astype(jnp.bfloat16)
    return (features, delta)


def pair_pool(queries, keys, values, head_bias):
    count = queries.shape[0]
    query_heads = queries.reshape(count, -1, DH)
    key_heads = keys.reshape(keys.shape[0], -1, DH)
    value_heads = values.reshape(values.shape[0], -1, DH)
    scores = jnp.einsum("phd,jhd->phj", query_heads, key_heads, preferred_element_type=jnp.float32)
    weights = jax.nn.silu(scores * (1.0 / math.sqrt(DH)) + head_bias[None, :, None]).astype(
        jnp.bfloat16
    )
    pooled = jnp.einsum("phj,jhd->phd", weights, value_heads, preferred_element_type=jnp.float32)
    return pooled.reshape(count, -1)


def on_device(
    particles,
    obs_embed,
    step_index,
    noise,
    w_query,
    w_key,
    w_value,
    w_time,
    w_score,
    prior_in,
    prior_time,
    prior_out,
):
    obs_count = lax.axis_size("obs")
    rep_count = lax.axis_size("rep")
    features, delta = plan(step_index, w_time.shape[0])
    head_bias = jnp.dot(features, w_time, preferred_element_type=jnp.float32)[0]
    keys = jnp.dot(obs_embed, w_key, preferred_element_type=jnp.float32).astype(jnp.bfloat16)
    values = jnp.dot(obs_embed, w_value, preferred_element_type=jnp.float32).astype(jnp.bfloat16)
    home = particles[0]
    block_rows = home.shape[0]
    width = home.shape[1]
    stripe = block_rows // obs_count
    owned = home.reshape(obs_count, stripe, width)
    theta_owner = lax.all_to_all(owned, "obs", split_axis=0, concat_axis=0, tiled=True)
    moving = home.astype(jnp.bfloat16)

    def pool(travel):
        queries = jnp.dot(travel, w_query, preferred_element_type=jnp.float32).astype(jnp.bfloat16)
        return pair_pool(queries, keys, values, head_bias)

    score_weight = w_score.astype(jnp.float32)

    def turn(turn_index, cycle_state):
        arrived = passed_along(cycle_state[0], "obs", 1)
        totals = passed_along(cycle_state[1], "obs", 1)
        return (arrived, totals + pool(arrived))

    cycle_state = lax.fori_loop(0, obs_count - 1, turn, (moving, pool(moving)))
    pieces = cycle_state[1].reshape(obs_count, stripe, -1)
    flat = pieces.reshape(-1, pieces.shape[-1])
    result = jnp.dot(
        flat, score_weight, precision=lax.Precision.HIGHEST, preferred_element_type=jnp.float32
    )
    pieces = result.reshape(pieces.shape[:-1] + (width,))
    received = lax.all_to_all(pieces, "obs", split_axis=0, concat_axis=0, tiled=True)
    summed = jnp.roll(received, 1, axis=0)
    owner_rows = theta_owner.reshape(block_rows, width)
    share = block_rows // rep_count
    start = lax.axis_index("rep") * share
    my_rows = lax.dynamic_slice_in_dim(owner_rows, start, share, 0).astype(jnp.bfloat16)
    prior_pre = jnp.dot(my_rows, prior_in, preferred_element_type=jnp.float32) + jnp.dot(
        features, prior_time, preferred_element_type=jnp.float32
    )
    prior_hidden = jax.nn.silu(prior_pre).astype(jnp.bfloat16)
    prior_part = jnp.dot(prior_hidden, prior_out, preferred_element_type=jnp.float32)
    total_count = obs_embed.shape[0] * obs_count * rep_count
    scores_flat = summed.reshape(block_rows, width)
    current = lax.dynamic_slice_in_dim(scores_flat, start, share, 0)
    scores_flat = lax.dynamic_update_slice_in_dim(
        scores_flat, current - (total_count - 1) * prior_part, start, 0
    )
    score_total = lax.psum(scores_flat, ("hid", "rep")).reshape(obs_count, stripe, width)
    updated = theta_owner + delta * score_total + jnp.sqrt(delta) * noise
    return (updated, score_total)


def solution(mesh):
    in_specs = (
        P(("groups", "obs"), None, None),
        P(("groups", "obs", "rep"), None),
        P("groups"),
        P("groups", "obs", None),
        P(None, "hid"),
        P(None, "hid"),
        P(None, "hid"),
        P(None, "hid"),
        P("hid", None),
        P(None, "hid"),
        P(None, "hid"),
        P("hid", None),
    )
    out_specs = (P("groups", "obs", None), P("groups", "obs", None))
    return jax.shard_map(
        on_device, mesh=mesh, in_specs=in_specs, out_specs=out_specs, check_vma=False
    )
```

profile of v0, /device:TPU:0, one launch (start us, length us, event | category | flops | bytes accessed | tf_op | source)
XLA Modules:
  0.0 154.7 jit_solution(1549332694135412617)
XLA Ops:
  8.1 0.3 copy-done
  8.4 4.3 %convolution_convert_fusion.2 = bf16[2048,1024]{0,1:T(8,128)(2,1)} fusion(bf16[2048,256]{1,0:T(8,128)(2,1)S(1)} %copy-done, bf16[256,1024]{1,0:T(8,128)(2,1)} %param.20), kind=kOutput, calls=%fused_computation.23 | convolution fusion | flops 1075838976 | bytes 5767168 | tf_op jit(solution)/shard_map/dot_general | solution.py:63
  12.8 3.3 %convolution_convert_fusion.1 = bf16[2048,1024]{0,1:T(8,128)(2,1)} fusion(bf16[2048,256]{1,0:T(8,128)(2,1)S(1)} %copy-done, bf16[256,1024]{1,0:T(8,128)(2,1)S(1)} %copy-done.4), kind=kOutput, calls=%fused_computation.22 | convolution fusion | flops 1075838976 | bytes 5767168 | tf_op jit(solution)/shard_map/dot_general | solution.py:62
  16.1 6.5 %copy.19 = bf16[2048,1024]{1,0:T(8,128)(2,1)} copy(bf16[2048,1024]{0,1:T(8,128)(2,1)} %convolution_convert_fusion.1) | data formatting | bytes 8388608 | tf_op jit(solution)/shard_map/while | solution.py:83
  22.7 0.3 fusion.21
  23.0 8.8 %fusion.20 = f32[8,128,128]{2,1,0:T(8,128)} fusion(bf16[2048,8,128]{0,2,1:T(8,128)(2,1)} %bitcast.116, bf16[2048,8,128]{0,2,1:T(8,128)(2,1)} %bitcast.115, f32[8]{0:T(128)S(1)} %bitcast.124, bf16[16,8,8,128]{3,2,1,0:T(8,128)(2,1)S(1)} %fusion.21), kind=kOutput, calls=%fused_computation.24 | convolution fusion | flops 1088421888 | bytes 9175072 | tf_op jit(solution)/shard_map/phj,jhd->phd/dot_general | solution.py:40
  31.9 56.9 %while.12 = (s32[]{:T(128)}, bf16[128,512]{1,0:T(8,128)(2,1)S(1)}, f32[128,1024]{0,1:T(8,128)}, bf16[512,1024]{1,0:T(8,128)(2,1)S(1)}, bf16[2048,1024]{1,0:T(8,1...) while((s32[]{:T(128)}, bf16[128,512]{1,0:T(8,128)(2,1)S(1)}, ...), condition=%wide.region_1.2_spmd, body=%wide.region_0.1_spmd.sunk | while | flops 1222901760 | bytes 15073477 | solution.py:83
  31.9 3.0 %collective-permute-start = (bf16[128,512]{1,0:T(8,128)(2,1)S(1)}, bf16[128,512]{1,0:T(8,128)(2,1)S(1)}, u32[]{:S(2)}, u32[]{:S(2)}) collective-permute-start(bf16[128,512]{1,0:T(8,128)(2,1)S(1)} %get-tuple-element.115), channel_id=1, source_target_pairs={{0,4},{4,8},{8,12},{12,0},{1,5},{5,9},{9,13},{13,1},{2,6},{6,10},{... | collective-permute-start | bytes 393224 | tf_op jit(solution)/shard_map/while/body/eval_jaxpr/ppermute | solution.py:15
  34.9 1.6 %collective-permute-start.1 = (f32[128,1024]{0,1:T(8,128)}, f32[128,1024]{0,1:T(8,128)S(1)}, u32[]{:S(2)}, u32[]{:S(2)}) collective-permute-start(f32[128,1024]{0,1:T(8,128)} %get-tuple-element.116), channel_id=1, source_target_pairs={{0,4},{4,8},{8,12},{12,0},{1,5},{5,9},{9,13},{13,1},{2,6},{6,10},{... | collective-permute-start | bytes 1572872 | tf_op jit(solution)/shard_map/while/body/eval_jaxpr/ppermute | solution.py:15
  36.5 4.8 %collective-permute-done = bf16[128,512]{1,0:T(8,128)(2,1)S(1)} collective-permute-done((bf16[128,512]{1,0:T(8,128)(2,1)S(1)}, bf16[128,512]{1,0:T(8,128)(2,1)S(1)}, u32[]{:S(2)}, u32[]{:S(2)}) %collective-permute-start) | collective-permute-done | bytes 131104 | tf_op jit(solution)/shard_map/while/body/eval_jaxpr/ppermute | solution.py:15
  41.6 6.3 %fusion.73 = f32[8,128,128]{1,2,0:T(8,128)S(1)} fusion(bf16[2048,8,128]{0,2,1:T(8,128)(2,1)} %bitcast.117, f32[8]{0:T(128)S(1)} %bitcast.125, bf16[16,8,8,128]{3,2,1,0:T(8,128)(2,1)S(1)} %fusion.72, bf16[2048,1024]{1,0:T(8,128)(2,1)} %get-tuple-element.126), kind=kOutput, calls=%fused_computation.8.clone.1 | convolution fusion | flops 1088421888 | bytes 9175072 | tf_op jit(solution)/shard_map/while/body/eval_jaxpr/phj,jhd->phd/dot_general | solution.py:40
  47.9 3.8 %collective-permute-done.1 = f32[128,1024]{0,1:T(8,128)S(1)} collective-permute-done((f32[128,1024]{0,1:T(8,128)}, f32[128,1024]{0,1:T(8,128)S(1)}, u32[]{:S(2)}, u32[]{:S(2)}) %collective-permute-start.1) | collective-permute-done | bytes 524320 | tf_op jit(solution)/shard_map/while/body/eval_jaxpr/ppermute | solution.py:15
  51.6 0.9 bitcast_add_fusion.2
  52.5 1.3 collective-permute-start.1
  53.8 6.9 %collective-permute-done = bf16[128,512]{1,0:T(8,128)(2,1)S(1)} collective-permute-done((bf16[128,512]{1,0:T(8,128)(2,1)S(1)}, bf16[128,512]{1,0:T(8,128)(2,1)S(1)}, u32[]{:S(2)}, u32[]{:S(2)}) %collective-permute-start) | collective-permute-done | bytes 131104 | tf_op jit(solution)/shard_map/while/body/eval_jaxpr/ppermute | solution.py:15
  61.1 6.3 %fusion.73 = f32[8,128,128]{1,2,0:T(8,128)S(1)} fusion(bf16[2048,8,128]{0,2,1:T(8,128)(2,1)} %bitcast.117, f32[8]{0:T(128)S(1)} %bitcast.125, bf16[16,8,8,128]{3,2,1,0:T(8,128)(2,1)S(1)} %fusion.72, bf16[2048,1024]{1,0:T(8,128)(2,1)} %get-tuple-element.126), kind=kOutput, calls=%fused_computation.8.clone.1 | convolution fusion | flops 1088421888 | bytes 9175072 | tf_op jit(solution)/shard_map/while/body/eval_jaxpr/phj,jhd->phd/dot_general | solution.py:40
  67.4 2.9 %collective-permute-done.1 = f32[128,1024]{0,1:T(8,128)S(1)} collective-permute-done((f32[128,1024]{0,1:T(8,128)}, f32[128,1024]{0,1:T(8,128)S(1)}, u32[]{:S(2)}, u32[]{:S(2)}) %collective-permute-start.1) | collective-permute-done | bytes 524320 | tf_op jit(solution)/shard_map/while/body/eval_jaxpr/ppermute | solution.py:15
  70.2 0.9 bitcast_add_fusion.2
  71.1 8.2 %collective-permute-done = bf16[128,512]{1,0:T(8,128)(2,1)S(1)} collective-permute-done((bf16[128,512]{1,0:T(8,128)(2,1)S(1)}, bf16[128,512]{1,0:T(8,128)(2,1)S(1)}, u32[]{:S(2)}, u32[]{:S(2)}) %collective-permute-start) | collective-permute-done | bytes 131104 | tf_op jit(solution)/shard_map/while/body/eval_jaxpr/ppermute | solution.py:15
  79.7 6.3 %fusion.73 = f32[8,128,128]{1,2,0:T(8,128)S(1)} fusion(bf16[2048,8,128]{0,2,1:T(8,128)(2,1)} %bitcast.117, f32[8]{0:T(128)S(1)} %bitcast.125, bf16[16,8,8,128]{3,2,1,0:T(8,128)(2,1)S(1)} %fusion.72, bf16[2048,1024]{1,0:T(8,128)(2,1)} %get-tuple-element.126), kind=kOutput, calls=%fused_computation.8.clone.1 | convolution fusion | flops 1088421888 | bytes 9175072 | tf_op jit(solution)/shard_map/while/body/eval_jaxpr/phj,jhd->phd/dot_general | solution.py:40
  86.0 2.0 %collective-permute-done.1 = f32[128,1024]{0,1:T(8,128)S(1)} collective-permute-done((f32[128,1024]{0,1:T(8,128)}, f32[128,1024]{0,1:T(8,128)S(1)}, u32[]{:S(2)}, u32[]{:S(2)}) %collective-permute-start.1) | collective-permute-done | bytes 524320 | tf_op jit(solution)/shard_map/while/body/eval_jaxpr/ppermute | solution.py:15
  87.9 0.9 bitcast_add_fusion.2
  88.8 2.2 %fusion.36 = f32[128,512]{1,0:T(8,128)S(1)} fusion(f32[128,1024]{0,1:T(8,128)} %get-tuple-element.39, bf16[1024,512]{1,0:T(8,128)(2,1)} %param.22), kind=kOutput, calls=%fused_computation.49 | convolution fusion | flops 805306368 | bytes 1835008 | tf_op jit(solution)/shard_map/dot_general | solution.py:86
  91.0 9.5 %all_to_all.10 = f32[4,32,512]{2,1,0:T(8,128)S(1)} all-to-all(f32[4,32,512]{2,1,0:T(8,128)S(1)} %bitcast.119), channel_id=1, replica_groups=mesh['groups'=2,'obs'=4,'hid'=2,'rep'=2] {'obs'}, dimensions={0} | all-to-all | bytes 524288 | tf_op jit(solution)/shard_map/all_to_all | solution.py:90
  100.5 3.4 %all-to-all-start = ((f32[4,32,512]{2,1,0:T(8,128)}), f32[4,32,512]{2,1,0:T(8,128)S(1)}, u32[]{:S(2)}, u32[]{:S(2)}) async-start(f32[4,32,512]{2,1,0:T(8,128)} %bitcast.120), calls=%async_computation | async-start | bytes 524288 | tf_op jit(solution)/shard_map/all_to_all | solution.py:69
  103.9 1.2 fusion.37
  105.2 5.4 %all-to-all-done = f32[4,32,512]{2,1,0:T(8,128)S(1)} async-done(((f32[4,32,512]{2,1,0:T(8,128)}), f32[4,32,512]{2,1,0:T(8,128)S(1)}, u32[]{:S(2)}, u32[]{:S(2)}) %all-to-all-start) | async-done | bytes 262176 | tf_op jit(solution)/shard_map/all_to_all | solution.py:69
  110.6 1.7 %fusion.23 = f32[128,512]{1,0:T(8,128)S(1)} fusion(f32[128,512]{1,0:T(8,128)S(1)} %bitcast.121, s32[]{:T(128)S(6)} %select_n.2, bf16[1024,512]{1,0:T(8,128)(2,1)S(1)} %copy-done.6, bf16[512,1024]{1,0:T(8,128)(2,1)} %param.23, f32[1024]{0:T(1024)S(1)} %bitcast.123, f32[128,512]{1,0:T(8,128)S(1)} %bitcast.118), kind=kOutput, calls=%fused_computation.30 | convolution fusion | flops 134676480 | bytes 2429952 | tf_op jit(solution)/shard_map/dot_general | solution.py:100
  112.4 0.7 copy-done.3
  113.2 31.3 %all-reduce.2.cloned.1.call-done = f32[4,32,512]{2,1,0:T(8,128)} async-done(((f32[4,32,512]{2,1,0:T(8,128)}), f32[4,32,512]{2,1,0:T(8,128)}) %all-reduce.2.cloned.1.call-update) | async-done | bytes 262160 | tf_op jit(solution)/shard_map/psum | solution.py:107
  144.5 1.7 %multiply_add_fusion = f32[4,32,512]{2,1,0:T(8,128)} fusion(f32[4,32,512]{2,1,0:T(8,128)S(1)} %copy-done.5, f32[4,32,512]{2,1,0:T(8,128)S(1)} %all-to-all-done, f32[4,32,512]{2,1,0:T(8,128)} %all-reduce.2.cloned.1.call-done, f32[]{:T(128)S(6)} %sqrt.3, f32[]{:T(128)} %bitcast.6), kind=kLoop, calls=%fused_computation.34 | loop fusion | flops 262144 | bytes 1048584 | tf_op jit(solution)/shard_map/add | solution.py:108
  146.2 1.7 %copy.57 = f32[4,32,512]{2,1,0:T(8,128)} copy(f32[4,32,512]{2,1,0:T(8,128)} %all-reduce.2.cloned.1.call-done) | data formatting | bytes 524288
  (33 shorter events, 1.3 us)
Async XLA Ops:
  7.2 1.2 copy-start
  8.4 4.4 %copy-start.4 = (bf16[256,1024]{1,0:T(8,128)(2,1)S(1)}, bf16[256,1024]{1,0:T(8,128)(2,1)}, u32[]{:S(2)}) copy-start(bf16[256,1024]{1,0:T(8,128)(2,1)} %param.19) | copy-start | bytes 1572868
  12.8 3.3 %copy-start.2 = (f32[1,128,512]{2,1,0:T(8,128)S(1)}, f32[1,128,512]{2,1,0:T(8,128)}, u32[]{:S(2)}) copy-start(f32[1,128,512]{2,1,0:T(8,128)} %param.14) | copy-start | bytes 786436
  16.1 6.5 %copy-start.7 = (bf16[256,8]{0,1:T(8,128)(2,1)S(1)}, bf16[256,8]{0,1:T(8,128)(2,1)}, u32[]{:S(2)}) copy-start(bf16[256,8]{0,1:T(8,128)(2,1)} %param.21) | copy-start | bytes 12292
  16.1 6.6 %copy-start.1 = (bf16[512,1024]{1,0:T(8,128)(2,1)S(1)}, bf16[512,1024]{1,0:T(8,128)(2,1)}, u32[]{:S(2)}) copy-start(bf16[512,1024]{1,0:T(8,128)(2,1)} %param.18) | copy-start | bytes 3145732
  31.9 9.4 %collective-permute-start = (bf16[128,512]{1,0:T(8,128)(2,1)S(1)}, bf16[128,512]{1,0:T(8,128)(2,1)S(1)}, u32[]{:S(2)}, u32[]{:S(2)}) collective-permute-start(bf16[128,512]{1,0:T(8,128)(2,1)S(1)} %get-tuple-element.115), channel_id=1, source_target_pairs={{0,4},{4,8},{8,12},{12,0},{1,5},{5,9},{9,13},{13,1},{2,6},{6,10},{... | collective-permute-start | bytes 393224 | tf_op jit(solution)/shard_map/while/body/eval_jaxpr/ppermute | solution.py:15
  34.9 16.7 %collective-permute-start.1 = (f32[128,1024]{0,1:T(8,128)}, f32[128,1024]{0,1:T(8,128)S(1)}, u32[]{:S(2)}, u32[]{:S(2)}) collective-permute-start(f32[128,1024]{0,1:T(8,128)} %get-tuple-element.116), channel_id=1, source_target_pairs={{0,4},{4,8},{8,12},{12,0},{1,5},{5,9},{9,13},{13,1},{2,6},{6,10},{... | collective-permute-start | bytes 1572872 | tf_op jit(solution)/shard_map/while/body/eval_jaxpr/ppermute | solution.py:15
  52.5 8.2 %collective-permute-start = (bf16[128,512]{1,0:T(8,128)(2,1)S(1)}, bf16[128,512]{1,0:T(8,128)(2,1)S(1)}, u32[]{:S(2)}, u32[]{:S(2)}) collective-permute-start(bf16[128,512]{1,0:T(8,128)(2,1)S(1)} %get-tuple-element.115), channel_id=1, source_target_pairs={{0,4},{4,8},{8,12},{12,0},{1,5},{5,9},{9,13},{13,1},{2,6},{6,10},{... | collective-permute-start | bytes 393224 | tf_op jit(solution)/shard_map/while/body/eval_jaxpr/ppermute | solution.py:15
  52.5 17.7 %collective-permute-start.1 = (f32[128,1024]{0,1:T(8,128)}, f32[128,1024]{0,1:T(8,128)S(1)}, u32[]{:S(2)}, u32[]{:S(2)}) collective-permute-start(f32[128,1024]{0,1:T(8,128)} %get-tuple-element.116), channel_id=1, source_target_pairs={{0,4},{4,8},{8,12},{12,0},{1,5},{5,9},{9,13},{13,1},{2,6},{6,10},{... | collective-permute-start | bytes 1572872 | tf_op jit(solution)/shard_map/while/body/eval_jaxpr/ppermute | solution.py:15
  71.1 8.2 %collective-permute-start = (bf16[128,512]{1,0:T(8,128)(2,1)S(1)}, bf16[128,512]{1,0:T(8,128)(2,1)S(1)}, u32[]{:S(2)}, u32[]{:S(2)}) collective-permute-start(bf16[128,512]{1,0:T(8,128)(2,1)S(1)} %get-tuple-element.115), channel_id=1, source_target_pairs={{0,4},{4,8},{8,12},{12,0},{1,5},{5,9},{9,13},{13,1},{2,6},{6,10},{... | collective-permute-start | bytes 393224 | tf_op jit(solution)/shard_map/while/body/eval_jaxpr/ppermute | solution.py:15
  71.1 16.8 %collective-permute-start.1 = (f32[128,1024]{0,1:T(8,128)}, f32[128,1024]{0,1:T(8,128)S(1)}, u32[]{:S(2)}, u32[]{:S(2)}) collective-permute-start(f32[128,1024]{0,1:T(8,128)} %get-tuple-element.116), channel_id=1, source_target_pairs={{0,4},{4,8},{8,12},{12,0},{1,5},{5,9},{9,13},{13,1},{2,6},{6,10},{... | collective-permute-start | bytes 1572872 | tf_op jit(solution)/shard_map/while/body/eval_jaxpr/ppermute | solution.py:15
  88.8 21.9 %copy-start.6 = (bf16[1024,512]{1,0:T(8,128)(2,1)S(1)}, bf16[1024,512]{1,0:T(8,128)(2,1)}, u32[]{:S(2)}) copy-start(bf16[1024,512]{1,0:T(8,128)(2,1)} %param.25) | copy-start | bytes 3145732
  88.8 55.7 %copy-start.5 = (f32[4,32,512]{2,1,0:T(8,128)S(1)}, f32[4,32,512]{2,1,0:T(8,128)}, u32[]{:S(2)}) copy-start(f32[4,32,512]{2,1,0:T(8,128)} %param.17) | copy-start | bytes 786436
  100.5 10.2 %all-to-all-start = ((f32[4,32,512]{2,1,0:T(8,128)}), f32[4,32,512]{2,1,0:T(8,128)S(1)}, u32[]{:S(2)}, u32[]{:S(2)}) async-start(f32[4,32,512]{2,1,0:T(8,128)} %bitcast.120), calls=%async_computation | async-start | bytes 524288 | tf_op jit(solution)/shard_map/all_to_all | solution.py:69
  103.9 40.6 %all-reduce.2.cloned.1.call-start = ((), (), s32[]{:S(2)}) async-start(), calls=%async_computation.2 | async-start | bytes 524288 | tf_op jit(solution)/shard_map/psum | solution.py:107
  112.4 0.7 copy-start.3
Sparse Core Ops, SparseCore 0:
  113.2 31.2 all-reduce.1
where the time goes:
time: 155 us
  waiting for transfers between devices  65.3 us (42%)
  matrix products  41.7 us (27%)
  between operations  15.1 us (10%)
  blocking collectives  9.51 us (6%)
  starting transfers between devices  9.34 us (6%)
  local copies, waits for them, and re-layouts  9.31 us (6%)
  other arithmetic  4.42 us (3%)
    psum x1, waiting for transfers between devices, on_device(): lax.psum(scores_flat, ('hid', 'rep')).reshape(obs_count, stripe, width)  31.3 us
    ppermute x6, waiting for transfers between devices, passed_along(): lax.ppermute(shard, axis, [(i, (i + by) % size) for i in range(size)])  28.5 us
    dot_general x4, matrix products, pair_pool(): jnp.einsum('phj,jhd->phd', weights, value_heads, preferred_element_type=j...  27.6 us
    all_to_all x1, blocking collectives, on_device(): lax.all_to_all(pieces, 'obs', split_axis=0, concat_axis=0, tiled=True)  9.51 us
    while x1, local copies, waits for them, and re-layouts, on_device(): cycle_state = lax.fori_loop(0, obs_count - 1, turn, (moving, pool(moving)))  6.51 us
    ppermute x6, starting transfers between devices, passed_along(): lax.ppermute(shard, axis, [(i, (i + by) % size) for i in range(size)])  5.89 us
    all_to_all x1, waiting for transfers between devices, on_device(): lax.all_to_all(owned, 'obs', split_axis=0, concat_axis=0, tiled=True)  5.4 us
    dot_general x1, matrix products, on_device(): jnp.dot(obs_embed, w_value, preferred_element_type=jnp.float32)  4.35 us
  transfers between devices with their start and end apart: 8, of which 8 were waited for; matrix products, arithmetic and copies ran while one was open for 14% of the time, Pallas kernels for 0%

commit v1 on v0

--- a/solution.py
+++ b/solution.py
@@ -87,7 +87,20 @@
         flat, score_weight, precision=lax.Precision.HIGHEST, preferred_element_type=jnp.float32
     )
     pieces = result.reshape(pieces.shape[:-1] + (width,))
-    received = lax.all_to_all(pieces, "obs", split_axis=0, concat_axis=0, tiled=True)
+    current_value = lax.axis_index("obs")
+    piece_now = lax.axis_size("obs")
+    z_new, spare = (piece_now, current_value)
+    front = pieces.shape[0] // z_new
+    v1 = list(pieces.shape)
+    v1[0] = front
+    response = v1[0]
+    v1[0] = response * z_new
+    received = jnp.zeros(v1, pieces.dtype)
+    for s in range(z_new):
+        aux = lax.dynamic_slice_in_dim(pieces, (spare ^ s) * front, front, axis=0)
+        if s:
+            aux = lax.ppermute(aux, "obs", [(d, d ^ s) for d in range(z_new)])
+        received = lax.dynamic_update_slice_in_dim(received, aux, (spare ^ s) * response, axis=0)
     summed = jnp.roll(received, 1, axis=0)
     owner_rows = theta_owner.reshape(block_rows, width)
     share = block_rows // rep_count

time: 155 us -> 150 us (0.968)
  blocking collectives: 9.51 us -> 0 us
  starting transfers between devices: 9.34 us -> 13.8 us
    all_to_all x1 -> x0, blocking collectives: 9.51 us -> none  [on_device(): lax.all_to_all(pieces, 'obs', split_axis=0, concat_axis=0, tiled=True)]
    ppermute x0 -> x3, starting transfers between devices: none -> 4.44 us  [on_device(): aux = lax.ppermute(aux, 'obs', [(d, d ^ s) for d in range(z_new)])]
  transfers between devices with their start and end apart: 8 -> 11, of which waited for: 8 -> 8; matrix products, arithmetic and copies ran while one was open for 14% -> 14% of each run, Pallas kernels for 0% -> 0%
where the time goes in v1:
time: 150 us
  waiting for transfers between devices  65.2 us (43%)
  matrix products  41.8 us (28%)
  between operations  15.1 us (10%)
  starting transfers between devices  13.8 us (9%)
  local copies, waits for them, and re-layouts  9.39 us (6%)
  other arithmetic  4.46 us (3%)
    psum x1, waiting for transfers between devices, on_device(): lax.psum(scores_flat, ('hid', 'rep')).reshape(obs_count, stripe, width)  31.3 us
    ppermute x6, waiting for transfers between devices, passed_along(): lax.ppermute(shard, axis, [(i, (i + by) % size) for i in range(size)])  28.5 us
    dot_general x4, matrix products, pair_pool(): jnp.einsum('phj,jhd->phd', weights, value_heads, preferred_element_type=j...  27.7 us
    while x1, local copies, waits for them, and re-layouts, on_device(): cycle_state = lax.fori_loop(0, obs_count - 1, turn, (moving, pool(moving)))  6.53 us
    ppermute x6, starting transfers between devices, passed_along(): lax.ppermute(shard, axis, [(i, (i + by) % size) for i in range(size)])  5.9 us
    all_to_all x1, waiting for transfers between devices, on_device(): lax.all_to_all(owned, 'obs', split_axis=0, concat_axis=0, tiled=True)  5.32 us
    ppermute x3, starting transfers between devices, on_device(): aux = lax.ppermute(aux, 'obs', [(d, d ^ s) for d in range(z_new)])  4.44 us
    dot_general x1, matrix products, on_device(): jnp.dot(obs_embed, w_value, preferred_element_type=jnp.float32)  4.36 us
  transfers between devices with their start and end apart: 11, of which 8 were waited for; matrix products, arithmetic and copies ran while one was open for 14% of the time, Pallas kernels for 0%

profile of v1, /device:TPU:0, one launch (start us, length us, event | category | flops | bytes accessed | tf_op | source)
XLA Modules:
  0.0 149.8 jit_solution(14334431264857857293)
XLA Ops:
  8.1 0.3 copy-done
  8.4 4.4 %convolution_convert_fusion.2 = bf16[2048,1024]{0,1:T(8,128)(2,1)} fusion(bf16[2048,256]{1,0:T(8,128)(2,1)S(1)} %copy-done, bf16[256,1024]{1,0:T(8,128)(2,1)} %param.20), kind=kOutput, calls=%fused_computation.23 | convolution fusion | flops 1075838976 | bytes 5767168 | tf_op jit(solution)/shard_map/dot_general | solution.py:63
  12.8 3.3 %convolution_convert_fusion.1 = bf16[2048,1024]{0,1:T(8,128)(2,1)} fusion(bf16[2048,256]{1,0:T(8,128)(2,1)S(1)} %copy-done, bf16[256,1024]{1,0:T(8,128)(2,1)S(1)} %copy-done.4), kind=kOutput, calls=%fused_computation.22 | convolution fusion | flops 1075838976 | bytes 5767168 | tf_op jit(solution)/shard_map/dot_general | solution.py:62
  16.1 6.5 %copy.19 = bf16[2048,1024]{1,0:T(8,128)(2,1)} copy(bf16[2048,1024]{0,1:T(8,128)(2,1)} %convolution_convert_fusion.1) | data formatting | bytes 8388608 | tf_op jit(solution)/shard_map/while | solution.py:83
  23.1 8.8 %fusion.20 = f32[8,128,128]{2,1,0:T(8,128)} fusion(bf16[2048,8,128]{0,2,1:T(8,128)(2,1)} %bitcast.116, bf16[2048,8,128]{0,2,1:T(8,128)(2,1)} %bitcast.115, f32[8]{0:T(128)S(1)} %bitcast.124, bf16[16,8,8,128]{3,2,1,0:T(8,128)(2,1)S(1)} %fusion.21), kind=kOutput, calls=%fused_computation.24 | convolution fusion | flops 1088421888 | bytes 9175072 | tf_op jit(solution)/shard_map/phj,jhd->phd/dot_general | solution.py:40
  31.9 56.9 %while.12 = (s32[]{:T(128)}, bf16[128,512]{1,0:T(8,128)(2,1)S(1)}, f32[128,1024]{0,1:T(8,128)}, bf16[512,1024]{1,0:T(8,128)(2,1)S(1)}, bf16[2048,1024]{1,0:T(8,1...) while((s32[]{:T(128)}, bf16[128,512]{1,0:T(8,128)(2,1)S(1)}, ...), condition=%wide.region_1.2_spmd, body=%wide.region_0.1_spmd.sunk | while | flops 1222901760 | bytes 15073477 | solution.py:83
  31.9 3.0 %collective-permute-start = (bf16[128,512]{1,0:T(8,128)(2,1)S(1)}, bf16[128,512]{1,0:T(8,128)(2,1)S(1)}, u32[]{:S(2)}, u32[]{:S(2)}) collective-permute-start(bf16[128,512]{1,0:T(8,128)(2,1)S(1)} %get-tuple-element.119), channel_id=1, source_target_pairs={{0,4},{4,8},{8,12},{12,0},{1,5},{5,9},{9,13},{13,1},{2,6},{6,10},{... | collective-permute-start | bytes 393224 | tf_op jit(solution)/shard_map/while/body/eval_jaxpr/ppermute | solution.py:15
  34.9 1.6 %collective-permute-start.1 = (f32[128,1024]{0,1:T(8,128)}, f32[128,1024]{0,1:T(8,128)S(1)}, u32[]{:S(2)}, u32[]{:S(2)}) collective-permute-start(f32[128,1024]{0,1:T(8,128)} %get-tuple-element.120), channel_id=1, source_target_pairs={{0,4},{4,8},{8,12},{12,0},{1,5},{5,9},{9,13},{13,1},{2,6},{6,10},{... | collective-permute-start | bytes 1572872 | tf_op jit(solution)/shard_map/while/body/eval_jaxpr/ppermute | solution.py:15
  36.5 4.8 %collective-permute-done = bf16[128,512]{1,0:T(8,128)(2,1)S(1)} collective-permute-done((bf16[128,512]{1,0:T(8,128)(2,1)S(1)}, bf16[128,512]{1,0:T(8,128)(2,1)S(1)}, u32[]{:S(2)}, u32[]{:S(2)}) %collective-permute-start) | collective-permute-done | bytes 131104 | tf_op jit(solution)/shard_map/while/body/eval_jaxpr/ppermute | solution.py:15
  41.6 6.3 %fusion.73 = f32[8,128,128]{1,2,0:T(8,128)S(1)} fusion(bf16[2048,8,128]{0,2,1:T(8,128)(2,1)} %bitcast.117, f32[8]{0:T(128)S(1)} %bitcast.125, bf16[16,8,8,128]{3,2,1,0:T(8,128)(2,1)S(1)} %fusion.72, bf16[2048,1024]{1,0:T(8,128)(2,1)} %get-tuple-element.130), kind=kOutput, calls=%fused_computation.8.clone.1 | convolution fusion | flops 1088421888 | bytes 9175072 | tf_op jit(solution)/shard_map/while/body/eval_jaxpr/phj,jhd->phd/dot_general | solution.py:40
  47.9 3.8 %collective-permute-done.1 = f32[128,1024]{0,1:T(8,128)S(1)} collective-permute-done((f32[128,1024]{0,1:T(8,128)}, f32[128,1024]{0,1:T(8,128)S(1)}, u32[]{:S(2)}, u32[]{:S(2)}) %collective-permute-start.1) | collective-permute-done | bytes 524320 | tf_op jit(solution)/shard_map/while/body/eval_jaxpr/ppermute | solution.py:15
  51.7 0.9 bitcast_add_fusion.2
  52.6 1.3 collective-permute-start.1
  53.9 6.9 %collective-permute-done = bf16[128,512]{1,0:T(8,128)(2,1)S(1)} collective-permute-done((bf16[128,512]{1,0:T(8,128)(2,1)S(1)}, bf16[128,512]{1,0:T(8,128)(2,1)S(1)}, u32[]{:S(2)}, u32[]{:S(2)}) %collective-permute-start) | collective-permute-done | bytes 131104 | tf_op jit(solution)/shard_map/while/body/eval_jaxpr/ppermute | solution.py:15
  60.8 0.3 fusion.72
  61.1 6.3 %fusion.73 = f32[8,128,128]{1,2,0:T(8,128)S(1)} fusion(bf16[2048,8,128]{0,2,1:T(8,128)(2,1)} %bitcast.117, f32[8]{0:T(128)S(1)} %bitcast.125, bf16[16,8,8,128]{3,2,1,0:T(8,128)(2,1)S(1)} %fusion.72, bf16[2048,1024]{1,0:T(8,128)(2,1)} %get-tuple-element.130), kind=kOutput, calls=%fused_computation.8.clone.1 | convolution fusion | flops 1088421888 | bytes 9175072 | tf_op jit(solution)/shard_map/while/body/eval_jaxpr/phj,jhd->phd/dot_general | solution.py:40
  67.4 2.9 %collective-permute-done.1 = f32[128,1024]{0,1:T(8,128)S(1)} collective-permute-done((f32[128,1024]{0,1:T(8,128)}, f32[128,1024]{0,1:T(8,128)S(1)}, u32[]{:S(2)}, u32[]{:S(2)}) %collective-permute-start.1) | collective-permute-done | bytes 524320 | tf_op jit(solution)/shard_map/while/body/eval_jaxpr/ppermute | solution.py:15
  70.3 0.9 bitcast_add_fusion.2
  71.2 8.2 %collective-permute-done = bf16[128,512]{1,0:T(8,128)(2,1)S(1)} collective-permute-done((bf16[128,512]{1,0:T(8,128)(2,1)S(1)}, bf16[128,512]{1,0:T(8,128)(2,1)S(1)}, u32[]{:S(2)}, u32[]{:S(2)}) %collective-permute-start) | collective-permute-done | bytes 131104 | tf_op jit(solution)/shard_map/while/body/eval_jaxpr/ppermute | solution.py:15
  79.7 6.3 %fusion.73 = f32[8,128,128]{1,2,0:T(8,128)S(1)} fusion(bf16[2048,8,128]{0,2,1:T(8,128)(2,1)} %bitcast.117, f32[8]{0:T(128)S(1)} %bitcast.125, bf16[16,8,8,128]{3,2,1,0:T(8,128)(2,1)S(1)} %fusion.72, bf16[2048,1024]{1,0:T(8,128)(2,1)} %get-tuple-element.130), kind=kOutput, calls=%fused_computation.8.clone.1 | convolution fusion | flops 1088421888 | bytes 9175072 | tf_op jit(solution)/shard_map/while/body/eval_jaxpr/phj,jhd->phd/dot_general | solution.py:40
  86.0 1.9 %collective-permute-done.1 = f32[128,1024]{0,1:T(8,128)S(1)} collective-permute-done((f32[128,1024]{0,1:T(8,128)}, f32[128,1024]{0,1:T(8,128)S(1)}, u32[]{:S(2)}, u32[]{:S(2)}) %collective-permute-start.1) | collective-permute-done | bytes 524320 | tf_op jit(solution)/shard_map/while/body/eval_jaxpr/ppermute | solution.py:15
  88.0 0.9 bitcast_add_fusion.2
  88.9 2.2 %fusion.36 = f32[128,512]{1,0:T(8,128)S(1)} fusion(f32[128,1024]{0,1:T(8,128)} %get-tuple-element.39, bf16[1024,512]{1,0:T(8,128)(2,1)} %param.22), kind=kOutput, calls=%fused_computation.56 | convolution fusion | flops 805306368 | bytes 1835008 | tf_op jit(solution)/shard_map/dot_general | solution.py:86
  91.4 4.2 %collective-permute-start.4 = (f32[1,32,512]{2,1,0:T(8,128)S(1)}, f32[1,32,512]{2,1,0:T(8,128)S(1)}, u32[]{:S(2)}, u32[]{:S(2)}) collective-permute-start(f32[1,32,512]{2,1,0:T(8,128)S(1)} %get-tuple-element.61), channel_id=1, source_target_pairs={{0,12},{4,8},{8,4},{12,0},{1,13},{5,9},{9,5},{13,1},{2,14},{6,10},... | collective-permute-start | bytes 196616 | tf_op jit(solution)/shard_map/ppermute | solution.py:102
  95.6 3.4 %all-to-all-start = ((f32[4,32,512]{2,1,0:T(8,128)}), f32[4,32,512]{2,1,0:T(8,128)S(1)}, u32[]{:S(2)}, u32[]{:S(2)}) async-start(f32[4,32,512]{2,1,0:T(8,128)} %bitcast.120), calls=%async_computation | async-start | bytes 524288 | tf_op jit(solution)/shard_map/all_to_all | solution.py:69
  99.0 1.2 fusion.37
  100.4 5.3 %all-to-all-done = f32[4,32,512]{2,1,0:T(8,128)S(1)} async-done(((f32[4,32,512]{2,1,0:T(8,128)}), f32[4,32,512]{2,1,0:T(8,128)S(1)}, u32[]{:S(2)}, u32[]{:S(2)}) %all-to-all-start) | async-done | bytes 262176 | tf_op jit(solution)/shard_map/all_to_all | solution.py:69
  105.7 1.7 %fusion.23 = f32[128,512]{1,0:T(8,128)S(1)} fusion(f32[128,512]{1,0:T(8,128)S(1)} %bitcast.121, s32[]{:T(128)S(6)} %select_n.25, bf16[1024,512]{1,0:T(8,128)(2,1)S(1)} %copy-done.6, bf16[512,1024]{1,0:T(8,128)(2,1)} %param.23, f32[1024]{0:T(1024)S(1)} %bitcast.123, f32[128,512]{1,0:T(8,128)S(1)} %bitcast.118), kind=kOutput, calls=%fused_computation.30 | convolution fusion | flops 134676480 | bytes 2429952 | tf_op jit(solution)/shard_map/dot_general | solution.py:113
  107.5 0.7 copy-done.3
  108.3 31.3 %all-reduce.2.cloned.1.call-done = f32[4,32,512]{2,1,0:T(8,128)} async-done(((f32[4,32,512]{2,1,0:T(8,128)}), f32[4,32,512]{2,1,0:T(8,128)}) %all-reduce.2.cloned.1.call-update) | async-done | bytes 262160 | tf_op jit(solution)/shard_map/psum | solution.py:120
  139.6 1.7 %multiply_add_fusion = f32[4,32,512]{2,1,0:T(8,128)} fusion(f32[4,32,512]{2,1,0:T(8,128)S(1)} %copy-done.5, f32[4,32,512]{2,1,0:T(8,128)S(1)} %all-to-all-done, f32[4,32,512]{2,1,0:T(8,128)} %all-reduce.2.cloned.1.call-done, f32[]{:T(128)S(6)} %sqrt.3, f32[]{:T(128)} %bitcast.6), kind=kLoop, calls=%fused_computation.34 | loop fusion | flops 262144 | bytes 1048584 | tf_op jit(solution)/shard_map/add | solution.py:121
  141.3 1.7 %copy.61 = f32[4,32,512]{2,1,0:T(8,128)} copy(f32[4,32,512]{2,1,0:T(8,128)} %all-reduce.2.cloned.1.call-done) | data formatting | bytes 524288
  (43 shorter events, 1.7 us)
Async XLA Ops:
  7.2 1.2 copy-start
  8.4 4.4 %copy-start.4 = (bf16[256,1024]{1,0:T(8,128)(2,1)S(1)}, bf16[256,1024]{1,0:T(8,128)(2,1)}, u32[]{:S(2)}) copy-start(bf16[256,1024]{1,0:T(8,128)(2,1)} %param.19) | copy-start | bytes 1572868
  12.8 3.3 %copy-start.2 = (f32[1,128,512]{2,1,0:T(8,128)S(1)}, f32[1,128,512]{2,1,0:T(8,128)}, u32[]{:S(2)}) copy-start(f32[1,128,512]{2,1,0:T(8,128)} %param.14) | copy-start | bytes 786436
  16.1 6.6 %copy-start.7 = (bf16[256,8]{0,1:T(8,128)(2,1)S(1)}, bf16[256,8]{0,1:T(8,128)(2,1)}, u32[]{:S(2)}) copy-start(bf16[256,8]{0,1:T(8,128)(2,1)} %param.21) | copy-start | bytes 12292
  16.1 6.7 %copy-start.1 = (bf16[512,1024]{1,0:T(8,128)(2,1)S(1)}, bf16[512,1024]{1,0:T(8,128)(2,1)}, u32[]{:S(2)}) copy-start(bf16[512,1024]{1,0:T(8,128)(2,1)} %param.18) | copy-start | bytes 3145732
  31.9 9.4 %collective-permute-start = (bf16[128,512]{1,0:T(8,128)(2,1)S(1)}, bf16[128,512]{1,0:T(8,128)(2,1)S(1)}, u32[]{:S(2)}, u32[]{:S(2)}) collective-permute-start(bf16[128,512]{1,0:T(8,128)(2,1)S(1)} %get-tuple-element.119), channel_id=1, source_target_pairs={{0,4},{4,8},{8,12},{12,0},{1,5},{5,9},{9,13},{13,1},{2,6},{6,10},{... | collective-permute-start | bytes 393224 | tf_op jit(solution)/shard_map/while/body/eval_jaxpr/ppermute | solution.py:15
  34.9 16.8 %collective-permute-start.1 = (f32[128,1024]{0,1:T(8,128)}, f32[128,1024]{0,1:T(8,128)S(1)}, u32[]{:S(2)}, u32[]{:S(2)}) collective-permute-start(f32[128,1024]{0,1:T(8,128)} %get-tuple-element.120), channel_id=1, source_target_pairs={{0,4},{4,8},{8,12},{12,0},{1,5},{5,9},{9,13},{13,1},{2,6},{6,10},{... | collective-permute-start | bytes 1572872 | tf_op jit(solution)/shard_map/while/body/eval_jaxpr/ppermute | solution.py:15
  52.6 8.2 %collective-permute-start = (bf16[128,512]{1,0:T(8,128)(2,1)S(1)}, bf16[128,512]{1,0:T(8,128)(2,1)S(1)}, u32[]{:S(2)}, u32[]{:S(2)}) collective-permute-start(bf16[128,512]{1,0:T(8,128)(2,1)S(1)} %get-tuple-element.119), channel_id=1, source_target_pairs={{0,4},{4,8},{8,12},{12,0},{1,5},{5,9},{9,13},{13,1},{2,6},{6,10},{... | collective-permute-start | bytes 393224 | tf_op jit(solution)/shard_map/while/body/eval_jaxpr/ppermute | solution.py:15
  52.6 17.7 %collective-permute-start.1 = (f32[128,1024]{0,1:T(8,128)}, f32[128,1024]{0,1:T(8,128)S(1)}, u32[]{:S(2)}, u32[]{:S(2)}) collective-permute-start(f32[128,1024]{0,1:T(8,128)} %get-tuple-element.120), channel_id=1, source_target_pairs={{0,4},{4,8},{8,12},{12,0},{1,5},{5,9},{9,13},{13,1},{2,6},{6,10},{... | collective-permute-start | bytes 1572872 | tf_op jit(solution)/shard_map/while/body/eval_jaxpr/ppermute | solution.py:15
  71.2 8.2 %collective-permute-start = (bf16[128,512]{1,0:T(8,128)(2,1)S(1)}, bf16[128,512]{1,0:T(8,128)(2,1)S(1)}, u32[]{:S(2)}, u32[]{:S(2)}) collective-permute-start(bf16[128,512]{1,0:T(8,128)(2,1)S(1)} %get-tuple-element.119), channel_id=1, source_target_pairs={{0,4},{4,8},{8,12},{12,0},{1,5},{5,9},{9,13},{13,1},{2,6},{6,10},{... | collective-permute-start | bytes 393224 | tf_op jit(solution)/shard_map/while/body/eval_jaxpr/ppermute | solution.py:15
  71.2 16.8 %collective-permute-start.1 = (f32[128,1024]{0,1:T(8,128)}, f32[128,1024]{0,1:T(8,128)S(1)}, u32[]{:S(2)}, u32[]{:S(2)}) collective-permute-start(f32[128,1024]{0,1:T(8,128)} %get-tuple-element.120), channel_id=1, source_target_pairs={{0,4},{4,8},{8,12},{12,0},{1,5},{5,9},{9,13},{13,1},{2,6},{6,10},{... | collective-permute-start | bytes 1572872 | tf_op jit(solution)/shard_map/while/body/eval_jaxpr/ppermute | solution.py:15
  88.9 16.9 %copy-start.6 = (bf16[1024,512]{1,0:T(8,128)(2,1)S(1)}, bf16[1024,512]{1,0:T(8,128)(2,1)}, u32[]{:S(2)}) copy-start(bf16[1024,512]{1,0:T(8,128)(2,1)} %param.25) | copy-start | bytes 3145732
  88.9 50.8 %copy-start.5 = (f32[4,32,512]{2,1,0:T(8,128)S(1)}, f32[4,32,512]{2,1,0:T(8,128)}, u32[]{:S(2)}) copy-start(f32[4,32,512]{2,1,0:T(8,128)} %param.17) | copy-start | bytes 786436
  91.1 9.1 %collective-permute-start.2 = (f32[1,32,512]{2,1,0:T(8,128)S(1)}, f32[1,32,512]{2,1,0:T(8,128)S(1)}, u32[]{:S(2)}, u32[]{:S(2)}) collective-permute-start(f32[1,32,512]{2,1,0:T(8,128)S(1)} %get-tuple-element.63), channel_id=1, source_target_pairs={{0,4},{4,0},{8,12},{12,8},{1,5},{5,1},{9,13},{13,9},{2,6},{6,2},{1... | collective-permute-start | bytes 196616 | tf_op jit(solution)/shard_map/ppermute | solution.py:102
  91.2 9.1 %collective-permute-start.3 = (f32[1,32,512]{2,1,0:T(8,128)S(1)}, f32[1,32,512]{2,1,0:T(8,128)S(1)}, u32[]{:S(2)}, u32[]{:S(2)}) collective-permute-start(f32[1,32,512]{2,1,0:T(8,128)S(1)} %get-tuple-element.62), channel_id=1, source_target_pairs={{0,8},{4,12},{8,0},{12,4},{1,9},{5,13},{9,1},{13,5},{2,10},{6,14},... | collective-permute-start | bytes 196616 | tf_op jit(solution)/shard_map/ppermute | solution.py:102
  91.4 8.9 %collective-permute-start.4 = (f32[1,32,512]{2,1,0:T(8,128)S(1)}, f32[1,32,512]{2,1,0:T(8,128)S(1)}, u32[]{:S(2)}, u32[]{:S(2)}) collective-permute-start(f32[1,32,512]{2,1,0:T(8,128)S(1)} %get-tuple-element.61), channel_id=1, source_target_pairs={{0,12},{4,8},{8,4},{12,0},{1,13},{5,9},{9,5},{13,1},{2,14},{6,10},... | collective-permute-start | bytes 196616 | tf_op jit(solution)/shard_map/ppermute | solution.py:102
  95.6 10.2 %all-to-all-start = ((f32[4,32,512]{2,1,0:T(8,128)}), f32[4,32,512]{2,1,0:T(8,128)S(1)}, u32[]{:S(2)}, u32[]{:S(2)}) async-start(f32[4,32,512]{2,1,0:T(8,128)} %bitcast.120), calls=%async_computation | async-start | bytes 524288 | tf_op jit(solution)/shard_map/all_to_all | solution.py:69
  99.0 40.6 %all-reduce.2.cloned.1.call-start = ((), (), s32[]{:S(2)}) async-start(), calls=%async_computation.1 | async-start | bytes 524288 | tf_op jit(solution)/shard_map/psum | solution.py:120
  107.4 0.7 copy-start.3
Sparse Core Ops, SparseCore 0:
  108.3 31.2 all-reduce.1
